TPU v7x, 128 devices: a whole 4x4x4 slice. The times are simulated.
128 devices in a mesh: src: 4 (over y), row: 32 (over x, z, core).
Axes of the slice: x: 4, y: 4, z: 4, core: 2. Of those that a mesh axis runs over, the one named last changes fastest.
Arguments:
- load_root: bfloat16 [8192, 1536], P('row', 'src'), may hold values from -48 to 48
- load_branch: bfloat16 [2, 8192, 1536], P(None, 'row', 'src'), may hold values from -48 to 48
- load_leaf: bfloat16 [4, 4096, 1536], P(None, 'row', 'src'), may hold values from -48 to 48
- inverse_root: bfloat16 [8192, 8192], P('row'), may hold values from -1.5 to 1.5, as said below
- inverse_branch: bfloat16 [2, 8192, 8192], P(None, 'row'), may hold values from -1.5 to 1.5, as said below
- inverse_leaf: bfloat16 [4, 4096, 4096], P(None, 'row'), may hold values from -1.5 to 1.5, as said below
- coupling_branch: bfloat16 [2, 2048, 8192], P(None, None, 'row'), may hold values from -0.0625 to 0.0625
- coupling_leaf: bfloat16 [4, 2048, 4096], P(None, None, 'row'), may hold values from -0.09375 to 0.09375
- blocks_branch: int32 [2, 16], replicated, may hold values from 0 to 63, as said below
- blocks_leaf: int32 [4, 16], replicated, may hold values from 0 to 127, as said below
- parents: int32 [4], replicated, may hold values from 0 to 1, as said below
Outputs:
- field_root: float32 [8192, 1536], P('row', 'src')
- field_branch: float32 [2, 8192, 1536], P(None, 'row', 'src')
- field_leaf: float32 [4, 4096, 1536], P(None, 'row', 'src')
- coverage_root: float32 [8192], P('row')
- coverage_branch: float32 [2, 8192], P(None, 'row')
- coverage_leaf: float32 [4, 4096], P(None, 'row')
Inputs may be any that keep to these rules, and one draw needn't show every extreme that they name: `inverse_root`: lower triangular; diagonal entries between 0.5 and 1.5. `inverse_branch`: each block lower triangular; diagonal entries between 0.5 and 1.5. `inverse_leaf`: each block lower triangular; diagonal entries between 0.5 and 1.5. `blocks_branch`: each row holds distinct root block numbers. `blocks_leaf`: each row holds distinct numbers; its first 8 entries are below 8192/128 (parent blocks), the others are 64 or more (root blocks). `parents`: each of the two level-1 separators is the parent of exactly two level-2 separators.
All inputs are finite; a program needn't handle non-finite values.
Results may differ from a plain program's by a relative error of at most 0.0055.
Values may be sent and summed in bfloat16 or wider, within the bound.
A program may use at most 128 MiB of HBM per device.

v0:
```python
import jax
import jax.numpy as jnp
from jax import lax
from jax.sharding import PartitionSpec as P

ROOT_ROWS = 8192
BRANCH_ROWS = 8192
BLOCK_ROWS = 128
COUPLE_BLOCKS = 16


def place_blocks(values, node_ids, blocks, keep_count, first_block, node_total):
    relative = blocks - first_block
    inside = (relative >= 0) & (relative < keep_count)
    target = jnp.where(inside, node_ids * keep_count + relative, node_total * keep_count)
    buckets = jnp.zeros((node_total * keep_count,) + values.shape[1:], jnp.float32)
    buckets = buckets.at[target].add(values, mode="drop")
    return buckets.reshape(node_total, keep_count * values.shape[1], values.shape[2])


def solve_piece(inverse, part_rows):
    return jnp.einsum("nrw,nwc->nrc", inverse, part_rows, preferred_element_type=jnp.float32)


def local(
    load_root,
    load_branch,
    load_leaf,
    inverse_root,
    inverse_branch,
    inverse_leaf,
    coupling_branch,
    coupling_leaf,
    blocks_branch,
    blocks_leaf,
    parents,
):
    row_count = lax.axis_size("row")
    rank_index = lax.axis_index("row")
    source_count = load_leaf.shape[2]
    half_count = COUPLE_BLOCKS // 2
    half_rows = half_count * BLOCK_ROWS
    branch_blocks = BRANCH_ROWS // BLOCK_ROWS
    root_blocks = ROOT_ROWS // BLOCK_ROWS
    root_inverse = inverse_root[None]
    root_load = load_root[None]
    field_leaf = solve_piece(inverse_leaf, lax.all_gather(load_leaf, "row", axis=1, tiled=True))
    leaf_terms = jnp.einsum(
        "nrw,nwc->nrc",
        coupling_leaf,
        field_leaf.astype(jnp.bfloat16),
        preferred_element_type=jnp.float32,
    )
    parent_nodes = jnp.repeat(parents, half_count)
    parent_blocks = blocks_leaf[:, :half_count].reshape(-1)
    upper_blocks = (blocks_leaf[:, half_count:] - branch_blocks).reshape(-1)
    branch_targets = blocks_branch.reshape(-1)
    leaf_total = lax.psum(leaf_terms, "row")
    to_parent = leaf_total[:, :half_rows]
    to_root = leaf_total[:, half_rows:]
    parent_values = to_parent.reshape(-1, BLOCK_ROWS, source_count)
    own_blocks = branch_blocks // row_count
    branch_update = place_blocks(
        parent_values, parent_nodes, parent_blocks, own_blocks, rank_index * own_blocks, 2
    )
    branch_y = (load_branch.astype(jnp.float32) - branch_update).astype(jnp.bfloat16)
    field_branch = solve_piece(inverse_branch, lax.all_gather(branch_y, "row", axis=1, tiled=True))
    branch_terms = jnp.einsum(
        "nrw,nwc->nrc",
        coupling_branch,
        field_branch.astype(jnp.bfloat16),
        preferred_element_type=jnp.float32,
    )
    branch_total = lax.psum(branch_terms, "row")
    root_values = jnp.concatenate(
        [
            to_root.reshape(-1, BLOCK_ROWS, source_count),
            branch_total.reshape(-1, BLOCK_ROWS, source_count),
        ],
        axis=0,
    )
    root_targets = jnp.concatenate([upper_blocks, branch_targets], axis=0)
    root_nodes = jnp.zeros(root_targets.shape, jnp.int32)
    own_root = root_blocks // row_count
    root_update = place_blocks(
        root_values, root_nodes, root_targets, own_root, rank_index * own_root, 1
    )
    root_y = (root_load.astype(jnp.float32) - root_update).astype(jnp.bfloat16)
    field_root = solve_piece(root_inverse, lax.all_gather(root_y, "row", axis=1, tiled=True))
    field_root = field_root[0]
    coverage_root, coverage_branch, coverage_leaf = lax.psum(
        (
            jnp.sum(field_root * field_root, axis=-1),
            jnp.sum(field_branch * field_branch, axis=-1),
            jnp.sum(field_leaf * field_leaf, axis=-1),
        ),
        "src",
    )
    return (field_root, field_branch, field_leaf, coverage_root, coverage_branch, coverage_leaf)


def solution(mesh):
    return jax.shard_map(
        local,
        mesh=mesh,
        in_specs=(
            P("row", "src"),
            P(None, "row", "src"),
            P(None, "row", "src"),
            P("row", None),
            P(None, "row", None),
            P(None, "row", None),
            P(None, None, "row"),
            P(None, None, "row"),
            P(),
            P(),
            P(),
        ),
        out_specs=(
            P("row", "src"),
            P(None, "row", "src"),
            P(None, "row", "src"),
            P("row"),
            P(None, "row"),
            P(None, "row"),
        ),
        check_vma=False,
    )
```

profile of v0, /device:TPU:0, one launch (start us, length us, event | category | flops | bytes accessed | tf_op | source)
XLA Modules:
  0.0 562.5 jit_solution(9774117825941916616)
XLA Ops:
  7.2 0.0 copy-start
  7.2 0.0 all-gather.5.cloned.1.call-start
  7.2 0.7 all-gather.5.cloned.1.call-update
  7.9 0.0 all-reduce.4.cloned.1.call-start
  8.0 67.8 %all-gather.5.cloned.1.call-done = bf16[4,4096,384]{2,1,0:T(8,128)(2,1)} async-done(((bf16[4,128,384]{2,1,0:T(8,128)(2,1)}), bf16[4,4096,384]{2,1,0:T(8,128)(2,1)}) %all-gather.5.cloned.1.call-update) | async-done | bytes 12582928 | tf_op jit(solution)/shard_map/all_gather | solution.py:47
  75.8 8.3 %multiply_reduce_fusion = (f32[4,128]{1,0:T(4,128)S(1)}, f32[4,128,384]{2,1,0:T(8,128)S(1)}) fusion(bf16[4,128,4096]{2,1,0:T(8,128)(2,1)} %param.16, bf16[4,4096,384]{2,1,0:T(8,128)(2,1)} %all-gather.5.cloned.1.call-done), kind=kOutput, calls=%fused_computation.7 | convolution fusion | flops 1611005440 | bytes 17565696 | tf_op jit(solution)/shard_map/nrw,nwc->nrc/dot_general | solution.py:22
  84.1 0.0 copy-start.2
  84.1 0.0 copy-done
  84.1 6.3 %convolution_bitcast_fusion = f32[4,2048,384]{1,2,0:T(8,128)} fusion(bf16[4,2048,128]{2,1,0:T(8,128)(2,1)S(1)} %copy-done, f32[4,128,384]{2,1,0:T(8,128)S(1)} %get-tuple-element.30), kind=kOutput, calls=%fused_computation.3 | convolution fusion | flops 805502976 | bytes 15466496 | tf_op jit(solution)/shard_map/nrw,nwc->nrc/dot_general | solution.py:48
  90.4 0.0 copy-done.2
  90.4 0.0 copy-start.8
  90.4 0.0 copy-start.6
  90.4 0.0 copy-start.4
  90.4 0.0 all-reduce.4.cloned.1.call-update
  90.4 0.0 all-gather.7.cloned.1.call-start
  90.5 0.6 copy-done.8
  91.1 0.0 copy-done.6
  91.1 0.1 add_select_fusion
  91.2 0.1 select_n.48
  91.3 0.2 copy-done.4
  91.4 0.2 copy.23
  91.6 131.3 %all-reduce.4.cloned.1.call-done = f32[4,2048,384]{1,2,0:T(8,128)} async-done(((f32[4,2048,384]{1,2,0:T(8,128)}), f32[4,2048,384]{1,2,0:T(8,128)}) %all-reduce.4.cloned.1.call-update) | async-done | bytes 12582928 | tf_op jit(solution)/shard_map/psum | solution.py:58
  223.0 11.8 %fusion.5 = (f32[4,1024,384]{1,2,0:T(8,128)}, f32[4,1024,384]{1,2,0:T(8,128)}) fusion(f32[4,2048,384]{1,2,0:T(8,128)} %all-reduce.4.cloned.1.call-done), kind=kLoop, calls=%fused_computation.25 | loop fusion | bytes 25165824 | tf_op jit(solution)/shard_map/slice | solution.py:60
  234.8 6.6 %copy.24 = f32[4,1024,384]{2,1,0:T(8,128)} copy(f32[4,1024,384]{1,2,0:T(8,128)} %get-tuple-element.22) | data formatting | bytes 12582912 | tf_op jit(solution)/shard_map/slice | solution.py:59
  241.4 0.1 broadcast_in_dim.22
  241.4 9.8 %scatter_fusion = f32[4,128,384]{2,1,0:T(8,128)S(1)} fusion(f32[4,128,384]{2,1,0:T(8,128)S(1)} %broadcast_in_dim.22, s32[32]{0:T(128)S(1)} %fusion.4, f32[32,128,384]{2,1,0:T(8,128)} %bitcast.31), kind=kCustom, calls=%fused_computation | custom fusion | flops 1572864 | bytes 18874496 | tf_op jit(solution)/shard_map/scatter-add | solution.py:17
  251.3 0.3 copy.25
  251.5 0.8 subtract_convert_fusion
  252.4 0.0 all-gather.7.cloned.1.call-update
  252.4 0.0 copy-start.3
  252.4 0.0 all-reduce.6.cloned.1.call-start
  252.5 69.1 %all-gather.7.cloned.1.call-done = bf16[2,8192,384]{1,2,0:T(8,128)(2,1)} async-done(((bf16[2,256,384]{1,2,0:T(8,128)(2,1)}), bf16[2,8192,384]{1,2,0:T(8,128)(2,1)}) %all-gather.7.cloned.1.call-update) | async-done | bytes 12582928 | tf_op jit(solution)/shard_map/all_gather | solution.py:67
  321.6 11.1 %multiply_reduce_fusion.1 = (f32[2,256]{1,0:T(2,128)S(1)}, f32[2,256,384]{1,2,0:T(8,128)S(1)}) fusion(bf16[2,8192,384]{1,2,0:T(8,128)(2,1)} %all-gather.7.cloned.1.call-done, bf16[2,256,8192]{2,1,0:T(8,128)(2,1)} %param.15), kind=kOutput, calls=%fused_computation.8 | convolution fusion | flops 3221618176 | bytes 21760000 | tf_op jit(solution)/shard_map/nrw,nwc->nrc/dot_general | solution.py:22
  332.7 0.0 copy-done.3
  332.7 3.7 convolution_bitcast_fusion.1
  336.3 6.6 %copy.26 = f32[2,2048,384]{2,1,0:T(8,128)} copy(f32[2,2048,384]{1,2,0:T(8,128)} %convolution_bitcast_fusion.1) | data formatting | bytes 12582912 | tf_op jit(solution)/shard_map/nrw,nwc->nrc/dot_general | solution.py:68
  342.9 0.0 copy-start.7
  342.9 0.0 all-reduce.6.cloned.1.call-update
  343.0 0.2 all-gather.9.cloned.1.call-start
  343.2 0.1 concatenate.17
  343.3 0.3 copy-done.7
  343.6 0.1 concatenate.18
  343.7 0.1 fusion.3
  343.8 6.6 %copy.22 = f32[4,1024,384]{2,1,0:T(8,128)} copy(f32[4,1024,384]{1,2,0:T(8,128)} %get-tuple-element.21) | data formatting | bytes 12582912 | tf_op jit(solution)/shard_map/slice | solution.py:60
  350.4 108.3 %all-reduce.6.cloned.1.call-done = f32[32,128,384]{2,1,0:T(8,128)} async-done(((f32[32,128,384]{2,1,0:T(8,128)}), f32[32,128,384]{2,1,0:T(8,128)}) %all-reduce.6.cloned.1.call-update) | async-done | bytes 6291472 | tf_op jit(solution)/shard_map/psum | solution.py:74
  458.7 10.6 %pad_maximum_fusion = f32[64,128,384]{2,1,0:T(8,128)} fusion(f32[32,128,384]{2,1,0:T(8,128)} %all-reduce.6.cloned.1.call-done, f32[32,128,384]{2,1,0:T(8,128)} %bitcast.30), kind=kLoop, calls=%fused_computation.2 | loop fusion | flops 3145728 | bytes 25165824 | tf_op jit(solution)/shard_map/concatenate | solution.py:75
  469.3 0.0 copy-start.5
  469.4 19.1 %scatter_fusion.1 = f32[2,128,384]{2,1,0:T(8,128)S(1)} fusion(f32[2,128,384]{2,1,0:T(8,128)S(1)} %broadcast_in_dim.21, s32[64]{0:T(128)S(1)} %fusion.3, f32[64,128,384]{2,1,0:T(8,128)} %pad_maximum_fusion), kind=kCustom, calls=%fused_computation.1 | custom fusion | flops 3145728 | bytes 37748992 | tf_op jit(solution)/shard_map/scatter-add | solution.py:17
  488.4 0.0 copy-done.5
  488.5 0.7 fusion
  489.2 0.0 all-gather.9.cloned.1.call-update
  489.2 0.0 copy-start.1
  489.2 1.1 copy.28
  490.4 47.7 %all-gather.9.cloned.1.call-done = bf16[8192,384]{1,0:T(8,128)(2,1)} async-done(((bf16[256,384]{1,0:T(8,128)(2,1)}), bf16[8192,384]{1,0:T(8,128)(2,1)}) %all-gather.9.cloned.1.call-update) | async-done | bytes 6291472 | tf_op jit(solution)/shard_map/all_gather | solution.py:89
  538.1 5.8 %multiply_reduce_fusion.2 = (f32[256]{0:T(256)S(1)}, f32[256,384]{0,1:T(8,128)S(1)}) fusion(bf16[8192,384]{1,0:T(8,128)(2,1)} %all-gather.9.cloned.1.call-done, bf16[256,8192]{1,0:T(8,128)(2,1)} %param.14), kind=kOutput, calls=%fused_computation.12 | convolution fusion | flops 1610809088 | bytes 10880000 | tf_op jit(solution)/shard_map/nrw,nwc->nrc/dot_general | solution.py:22
  543.9 0.9 copy.27
  544.8 11.1 %all-reduce = (f32[256]{0:T(256)}, f32[2,256]{1,0:T(2,128)}, f32[4,128]{1,0:T(4,128)}) all-reduce(f32[256]{0:T(256)S(1)} %get-tuple-element.25, f32[2,256]{1,0:T(2,128)S(1)} %get-tuple-element.27, f32[4,128]{1,0:T(4,128)S(1)} %get-tuple-element.29), channel_id=1, replica_groups=mesh['src'=4,'row'=32] {'src'}, use_global_device_ids=true, to_apply=%region_5.6 | all-reduce | flops 1280 | bytes 10240 | tf_op jit(solution)/shard_map/psum | solution.py:91
  555.9 0.0 copy-done.1
  (3 shorter events, 0.0 us)
Async XLA Ops:
  7.2 76.9 %copy-start = (bf16[4,2048,128]{2,1,0:T(8,128)(2,1)S(1)}, bf16[4,2048,128]{2,1,0:T(8,128)(2,1)}, u32[]{:S(2)}) copy-start(bf16[4,2048,128]{2,1,0:T(8,128)(2,1)} %param.18) | copy-start | bytes 6291460
  7.2 68.6 %all-gather.5.cloned.1.call-start = ((), (), s32[]{:S(2)}) async-start(), calls=%async_computation | async-start | bytes 12976128 | tf_op jit(solution)/shard_map/all_gather | solution.py:47
  7.9 215.0 %all-reduce.4.cloned.1.call-start = ((), (), s32[]{:S(2)}) async-start(), calls=%async_computation.1 | async-start | bytes 25165824 | tf_op jit(solution)/shard_map/psum | solution.py:58
  84.1 6.3 %copy-start.2 = (f32[4,128,384]{2,1,0:T(8,128)}, f32[4,128,384]{2,1,0:T(8,128)S(1)}, u32[]{:S(2)}) copy-start(f32[4,128,384]{2,1,0:T(8,128)S(1)} %get-tuple-element.30) | copy-start | bytes 2359300
  90.4 0.7 copy-start.8
  90.4 0.7 copy-start.6
  90.4 1.0 copy-start.4
  90.4 231.1 %all-gather.7.cloned.1.call-start = ((), (), s32[]{:S(2)}) async-start(), calls=%async_computation.2 | async-start | bytes 12976128 | tf_op jit(solution)/shard_map/all_gather | solution.py:67
  252.4 80.3 %copy-start.3 = (bf16[2,2048,256]{2,1,0:T(8,128)(2,1)S(1)}, bf16[2,2048,256]{2,1,0:T(8,128)(2,1)}, u32[]{:S(2)}) copy-start(bf16[2,2048,256]{2,1,0:T(8,128)(2,1)} %param.17) | copy-start | bytes 6291460
  252.4 206.3 %all-reduce.6.cloned.1.call-start = ((), (), s32[]{:S(2)}) async-start(), calls=%async_computation.3 | async-start | bytes 12582912 | tf_op jit(solution)/shard_map/psum | solution.py:74
  342.9 0.7 copy-start.7
  343.0 195.1 %all-gather.9.cloned.1.call-start = ((), (), s32[]{:S(2)}) async-start(), calls=%async_computation.4 | async-start | bytes 6488064 | tf_op jit(solution)/shard_map/all_gather | solution.py:89
  469.3 19.1 %copy-start.5 = (bf16[256,384]{1,0:T(8,128)(2,1)S(1)}, bf16[256,384]{1,0:T(8,128)(2,1)}, u32[]{:S(2)}) copy-start(bf16[256,384]{1,0:T(8,128)(2,1)} %param.11) | copy-start | bytes 589828
  489.2 66.7 %copy-start.1 = (bf16[4,2048,128]{2,1,0:T(8,128)(2,1)S(1)}, bf16[4,2048,128]{2,1,0:T(8,128)(2,1)}, u32[]{:S(2)}) copy-start(bf16[4,2048,128]{2,1,0:T(8,128)(2,1)} %param.18) | copy-start | bytes 6291460
Sparse Core Ops, SparseCore 0:
  10.3 65.4 all-gather.4
  90.6 132.3 all-reduce.3
  252.5 69.0 all-gather.6
  343.1 115.5 all-reduce.5
  489.3 48.6 all-gather.8
where the time goes:
time: 563 us; the launch traced here: 562 us
  waiting for transfers between devices  425 us (75%)
  other arithmetic  41.3 us (7%)
  local copies, waits for them, and re-layouts  35.6 us (6%)
  matrix products  35.2 us (6%)
  between operations  13.9 us (2%)
  blocking collectives  11.1 us (2%)
    psum x1, waiting for transfers between devices, local(): leaf_total = lax.psum(leaf_terms, 'row')  131 us
    psum x1, waiting for transfers between devices, local(): branch_total = lax.psum(branch_terms, 'row')  108 us
    all_gather x1, waiting for transfers between devices, local(): lax.all_gather(branch_y, 'row', axis=1, tiled=True)  69.1 us
    all_gather x1, waiting for transfers between devices, local(): lax.all_gather(load_leaf, 'row', axis=1, tiled=True)  67.8 us
    all_gather x1, waiting for transfers between devices, local(): lax.all_gather(root_y, 'row', axis=1, tiled=True)  47.7 us
    scatter-add x2, other arithmetic, place_blocks(): buckets = buckets.at[target].add(values, mode='drop')  28.9 us
    dot_general x3, matrix products, solve_piece(): jnp.einsum('nrw,nwc->nrc', inverse, part_rows, preferred_element_type=jnp...  25.2 us
    slice x2, local copies, waits for them, and re-layouts, local(): to_root = leaf_total[:, half_rows:]  18.5 us
  transfers between devices with their start and end apart: 5, of which 5 were waited for; matrix products, arithmetic and copies ran while one was open for 1% of the time, Pallas kernels for 0%

commit v1 on v0

v1 whole, which is shorter than its diff:
```python
import jax
import jax.numpy as jnp
from jax import lax
from jax.experimental import pallas as pl
from jax.experimental.pallas import tpu as pltpu
from jax.sharding import PartitionSpec as P

MESH = pl.DeviceIdType.MESH
F32 = jnp.float32
BF16 = jnp.bfloat16
OFFSETS = (0, -1, 1, 2)


class Place:
    def __init__(self):
        self.me = lax.axis_index("row")
        chip = self.me // 2
        self.core = lax.rem(self.me, 2)
        self.chip = chip
        self.x = chip // 4
        self.z = lax.rem(chip, 4)

    def row(self, dx, dz):
        x = lax.rem(self.x + (dx + 4), 4)
        z = lax.rem(self.z + (dz + 4), 4)
        return (x * 4 + z) * 2 + self.core

    def along(self, axis, d):
        return self.row(d, 0) if axis == "x" else self.row(0, d)

    def partner(self):
        return self.me + 1 - 2 * self.core

    def entry(self, extra=()):
        barrier = pltpu.get_barrier_semaphore()
        peers = [{"row": r} for r in (self.row(1, 0), self.row(-1, 0), self.row(0, 1), self.row(0, -1), self.partner())]
        peers += list(extra)
        for peer in peers:
            pl.semaphore_signal(barrier, inc=1, device_id=peer, device_id_type=MESH)
        pl.semaphore_wait(barrier, len(peers))


def push(src, dst, send, recv, row):
    pltpu.make_async_remote_copy(
        src_ref=src, dst_ref=dst, send_sem=send, recv_sem=recv, device_id={"row": row}, device_id_type=MESH
    ).start()


def await_bytes(ref, sem):
    pltpu.make_async_copy(ref, ref, sem).wait()


def gather(place, buf, own, send, recv, pair):
    axes = (("x", "z"), ("z", "x"))

    def owner(g, o1, o2):
        return place.row(o1, o2) if g == 0 else place.row(o2, o1)

    def piece(g, o1, o2, q0, q1):
        dst = buf.at[owner(g, o1, o2), 2 * g + q0 : 2 * g + q1]
        if (o1, o2) == (0, 0):
            return own.at[2 * g + q0 : 2 * g + q1], dst
        return dst, dst

    def slot(g, phase, o1, k):
        ring = 0 if phase == 1 else 1 + OFFSETS.index(o1)
        return recv.at[(g * 5 + ring) * 3 + k]

    def ring_send(g, phase, o1):
        src, dst = piece(g, o1, 0, 0, 2)
        for d, k in ((1, 0), (-1, 1)):
            push(src, dst, send, slot(g, phase, o1, k), place.along(axes[g][phase - 1], d))

    def to_partner(g, o1, o2):
        src, dst = piece(g, o1, o2, 0, 2)
        push(src, dst, send, pair, place.partner())

    def arrived(g, phase, o1, side):
        at = (side, 0) if phase == 1 else (o1, side)
        _, whole = piece(g, at[0], at[1], 0, 2)
        k = 0 if side == -1 else 1
        await_bytes(whole, slot(g, phase, o1, k))
        _, part = piece(g, at[0], at[1], k, k + 1)
        push(part, part, send, slot(g, phase, o1, 2), place.along(axes[g][phase - 1], -side))
        if phase == 1:
            ring_send(g, 2, side)
        to_partner(g, *at)

    def far(g, phase, o1):
        at = (2, 0) if phase == 1 else (o1, 2)
        _, whole = piece(g, at[0], at[1], 0, 2)
        await_bytes(whole, slot(g, phase, o1, 2))
        if phase == 1:
            ring_send(g, 2, 2)
        to_partner(g, *at)

    for g in (0, 1):
        ring_send(g, 1, 0)
    for g in (0, 1):
        ring_send(g, 2, 0)
        to_partner(g, 0, 0)
    yield
    events = []
    for side in (-1, 1):
        events += [(arrived, g, 1, 0, side) for g in (0, 1)]
    for side in (-1, 1):
        events += [(arrived, g, 2, 0, side) for g in (0, 1)]
    events += [(far, g, 1, 0) for g in (0, 1)]
    for o1 in (-1, 1):
        for side in (-1, 1):
            events += [(arrived, g, 2, o1, side) for g in (0, 1)]
    events += [(far, g, 2, 0) for g in (0, 1)]
    for side in (-1, 1):
        events += [(arrived, g, 2, 2, side) for g in (0, 1)]
    for o1 in (-1, 1, 2):
        events += [(far, g, 2, o1) for g in (0, 1)]
    for event in events:
        event[0](*event[1:])
        yield
    await_bytes(buf.at[0:16], pair)
    await_bytes(buf.at[0:31], send)
    yield


def reduce(place, s, t1, t2, t3, t4, out, send, recv):
    axes = (("x", "z"), ("z", "x"))

    def coord(axis, d):
        return lax.rem((place.x if axis == "x" else place.z) + (d + 4), 4)

    def line(g, d, q):
        a = coord(axes[g][0], d)
        return (a, slice(None), q) if g == 0 else (slice(None), a, q)

    def cell(g, d, q):
        a = coord(axes[g][0], 0)
        b = coord(axes[g][1], d)
        return (a, b, q) if g == 0 else (b, a, q)

    def both(g):
        return slice(2 * g, 2 * g + 2)

    def slot(g, k):
        return recv.at[g * 8 + k]

    for phase, index, ta, tb in ((0, line, t1, t2), (1, cell, t3, t4)):
        for g in (0, 1):
            axis = axes[g][phase]
            for k, d in ((0, -1), (1, 1)):
                push(s.at[index(g, 2 * d, 2 * g + k)], ta.at[g, k], send, slot(g, 4 * phase + k), place.along(axis, d))
        yield
        for g in (0, 1):
            axis = axes[g][phase]
            for k, d in ((0, -1), (1, 1)):
                await_bytes(ta.at[g, k], slot(g, 4 * phase + k))
                at = index(g, d, 2 * g + k)
                s[at] = (s[at].astype(F32) + ta[g, k].astype(F32)).astype(BF16)
                push(s.at[index(g, d, both(g))], tb.at[g, k], send, slot(g, 4 * phase + 2 + k), place.along(axis, d))
            yield
        for g in (0, 1):
            for k in (0, 1):
                await_bytes(tb.at[g, k], slot(g, 4 * phase + 2 + k))
            at = index(g, 0, both(g))
            total = s[at].astype(F32) + tb[g, 0].astype(F32) + tb[g, 1].astype(F32)
            if phase == 0:
                s[at] = total.astype(BF16)
            else:
                out[both(g)] = total.astype(BF16)
            yield


def couple(place, c_ref, z_ref, p_send, q_recv, s, send, recv, rows, per_node, pieces):
    step = 16 // pieces

    def product(owner):
        node = owner // per_node
        first = pl.multiple_of(lax.rem(owner, per_node) * rows, rows)
        return jnp.dot(c_ref[node, pl.ds(first, rows), :], z_ref[node], preferred_element_type=F32)

    shape = p_send.shape[1:]
    for piece in range(pieces):

        @pl.loop(piece * step, piece * step + step)
        def _(chip):
            p_send[chip] = product(chip * 2 + 1 - place.core).astype(BF16).reshape(shape)
            push(p_send.at[chip], q_recv.at[chip], send, recv.at[chip], place.partner())

        yield
    for piece in range(pieces):

        @pl.loop(piece * step, piece * step + step)
        def _(chip):
            await_bytes(q_recv.at[chip], recv.at[chip])
            other = q_recv[chip].reshape(rows, shape[2]).astype(F32)
            s[chip // 4, lax.rem(chip, 4)] = (product(chip * 2 + place.core) + other).astype(BF16).reshape(shape)

        yield


def drain(*tasks):
    for task in tasks:
        for _ in task:
            pass


def advance(task, count):
    for _ in range(count):
        if next(task, 0) == 0:
            return


def leaf_kernel(
    load_leaf, load_branch, load_root, inverse, coupling,
    field, b_branch, b_root, u_all,
    b, a, c, z, p_send, q_recv, s, t1, t2, t3, t4, u_own,
    send, recv_l, recv_b, recv_r, recv_u, pair, recv_s, recv_q, local,
):
    place = Place()
    me = place.me
    copies = [
        pltpu.make_async_copy(inverse, a, local.at[0]),
        pltpu.make_async_copy(coupling, c, local.at[1]),
        pltpu.make_async_copy(load_leaf, b.at[me], local.at[2]),
        pltpu.make_async_copy(load_branch, b_branch.at[me], local.at[3]),
        pltpu.make_async_copy(load_root, b_root.at[me], local.at[4]),
    ]
    for copy in copies:
        copy.start()
    place.entry()
    ag_leaf = gather(place, b, load_leaf, send.at[0], recv_l, pair.at[0])
    ag_branch = gather(place, b_branch, load_branch, send.at[1], recv_b, pair.at[1])
    ag_root = gather(place, b_root, load_root, send.at[2], recv_r, pair.at[2])
    ag_u = gather(place, u_all, u_own, send.at[3], recv_u, pair.at[3])
    advance(ag_leaf, 27)
    advance(ag_branch, 1)
    for copy in copies[:3]:
        copy.wait()
    drain(ag_leaf)

    def leaf():
        for n in range(4):
            field[n] = jnp.zeros_like(field.at[n])

            @pl.loop(0, place.chip // 4 + 1)
            def _(j):
                cols = pl.ds(pl.multiple_of(j * 1024, 1024), 1024)
                rows = b[pl.ds(j * 8, 8), n].reshape(1024, b.shape[3])
                field[n] += jnp.dot(a[n, :, cols], rows, preferred_element_type=F32)

            z[n] = field[n].astype(BF16)
            yield
        yield from couple(place, c, z, p_send, q_recv, s, send.at[4], recv_q, 256, 8, 4)

    for _ in leaf():
        advance(ag_branch, 1)
    rs = reduce(place, s, t1, t2, t3, t4, u_own, send.at[4], recv_s)
    for _ in rs:
        advance(ag_branch, 2)
    mine = pltpu.make_async_copy(u_own, u_all.at[me], local.at[5])
    mine.start()
    advance(ag_u, 1)
    drain(ag_branch)
    advance(ag_root, 1)
    for _ in ag_u:
        advance(ag_root, 1)
    drain(ag_root)
    await_bytes(u_all.at[0:31], send.at[4])
    mine.wait()
    for copy in copies[3:]:
        copy.wait()


def correct(out, index, a_cols, ids, u_rows, ag):
    for k in range(8):
        ag[:, k * 128 : k * 128 + 128] = a_cols(pl.multiple_of(ids(k) * 128, 128))
    out[index] -= jnp.dot(ag[...], u_rows.reshape(1024, u_rows.shape[-1]), preferred_element_type=F32)


def branch_kernel(
    blocks_leaf, parents, a_branch, b_branch, u_all,
    field, z,
    ab, bb, ul, ag, sems,
):
    width = bb.shape[3]
    copies = []
    for j in range(8):
        cols = slice(1024 * j, 1024 * j + 1024)
        copies.append(pltpu.make_async_copy(b_branch.at[4 * j : 4 * j + 4], bb.at[4 * j : 4 * j + 4], sems.at[2 * j]))
        copies.append(pltpu.make_async_copy(a_branch.at[:, :, cols], ab.at[:, :, cols], sems.at[2 * j + 1]))
    for i in range(4):
        copies.append(pltpu.make_async_copy(u_all.at[8 * i : 8 * i + 4], ul.at[i], sems.at[16 + i]))
    for copy in copies:
        copy.start()
    trips = lax.axis_index("row") // 4 + 1
    field[...] = jnp.zeros_like(field)
    for j in range(8):
        copies[2 * j].wait()
        copies[2 * j + 1].wait()

        @pl.when(j < trips)
        def _():
            for n in range(2):
                rows = bb[4 * j : 4 * j + 4, 2 * n : 2 * n + 2].reshape(1024, width)
                field[n] += jnp.dot(ab[n, :, 1024 * j : 1024 * j + 1024], rows, preferred_element_type=F32)

    for copy in copies[16:]:
        copy.wait()

    @pl.loop(0, 4)
    def _(i):
        n = parents[i]
        correct(field, n, lambda col: ab[n, :, pl.ds(col, 128)], lambda k: blocks_leaf[i, k], ul[i], ag)

    z[...] = field[...].astype(BF16)


def upper_kernel(
    z_in, c_branch, a_root, b_root,
    field_root, u2,
    zb, cb, ar, br, p_send, q_recv, s, t1, t2, t3, t4, u_own,
    send, recv_u, pair, recv_s, recv_q, local,
):
    place = Place()
    me = place.me
    width = br.shape[3]
    pairs = ((z_in, zb), (c_branch, cb), (b_root, br), (a_root, ar))
    copies = [pltpu.make_async_copy(src, dst, local.at[k]) for k, (src, dst) in enumerate(pairs)]
    for copy in copies:
        copy.start()
    place.entry()
    copies[0].wait()
    copies[1].wait()
    drain(couple(place, cb, zb, p_send, q_recv, s, send.at[0], recv_q, 128, 16, 1))

    def root():
        trips = me // 4 + 1
        copies[2].wait()
        copies[3].wait()
        field_root[...] = jnp.zeros_like(field_root)
        for h in range(4):

            @pl.loop(jnp.minimum(trips, 2 * h), jnp.minimum(trips, 2 * h + 2))
            def _(j):
                cols = pl.ds(pl.multiple_of(j * 1024, 1024), 1024)
                rows = br[pl.ds(j * 4, 4)].reshape(1024, width)
                field_root[...] += jnp.dot(ar[:, cols], rows, preferred_element_type=F32)

            yield

    work = root()
    rs = reduce(place, s, t1, t2, t3, t4, u_own, send.at[0], recv_s)
    for _ in rs:
        advance(work, 1)
    drain(work)
    mine = pltpu.make_async_copy(u_own, u2.at[me], local.at[4])
    mine.start()
    drain(gather(place, u2, u_own, send.at[1], recv_u, pair.at[0]))
    await_bytes(u2.at[0:31], send.at[0])
    mine.wait()


def root_kernel(
    blocks_branch, blocks_leaf, a_root, u_all, u2_in, partial,
    field,
    ar, ul, ub, ag, sems,
):
    copies = [pltpu.make_async_copy(a_root, ar, sems.at[0]), pltpu.make_async_copy(u2_in, ub, sems.at[1])]
    for i in range(4):
        copies.append(pltpu.make_async_copy(u_all.at[8 * i + 4 : 8 * i + 8], ul.at[i], sems.at[2 + i]))
    for copy in copies:
        copy.start()
    field[...] = partial[...]
    for copy in copies:
        copy.wait()

    @pl.loop(0, 4)
    def _(i):
        correct(field, ..., lambda col: ar[:, pl.ds(col, 128)], lambda k: blocks_leaf[i, 8 + k] - 64, ul[i], ag)

    @pl.loop(0, 4)
    def _(i):
        p, h = i // 2, lax.rem(i, 2)
        rows = ub[pl.ds(i * 8, 8)]
        correct(field, ..., lambda col: ar[:, pl.ds(col, 128)], lambda k: blocks_branch[p, 8 * h + k], rows, ag)


def reduce_scratch(q, c):
    return [
        pltpu.VMEM((16, 4, q, c), BF16),
        pltpu.VMEM((16, 4, q, c), BF16),
        pltpu.VMEM((4, 4, 4, q, c), BF16),
        pltpu.VMEM((2, 2, 4, q, c), BF16),
        pltpu.VMEM((2, 2, 4, 2, q, c), BF16),
        pltpu.VMEM((2, 2, q, c), BF16),
        pltpu.VMEM((2, 2, 2, q, c), BF16),
        pltpu.VMEM((4, q, c), BF16),
    ]


def local(
    load_root, load_branch, load_leaf, inverse_root, inverse_branch, inverse_leaf,
    coupling_branch, coupling_leaf, blocks_branch, blocks_leaf, parents,
):
    c = load_leaf.shape[2]
    dma = pltpu.SemaphoreType.DMA
    anywhere = pl.BlockSpec(memory_space=pl.ANY)
    vmem = pl.BlockSpec(memory_space=pltpu.VMEM)
    smem = pl.BlockSpec(memory_space=pltpu.SMEM)
    field_leaf, b_branch, b_root, u_all = pl.pallas_call(
        leaf_kernel,
        out_shape=(
            jax.ShapeDtypeStruct((4, 128, c), F32),
            jax.ShapeDtypeStruct((32, 4, 128, c), BF16),
            jax.ShapeDtypeStruct((32, 4, 64, c), BF16),
            jax.ShapeDtypeStruct((32, 4, 64, c), BF16),
        ),
        in_specs=[anywhere] * 5,
        out_specs=(vmem, anywhere, anywhere, anywhere),
        scratch_shapes=[
            pltpu.VMEM((32, 4, 128, c), BF16),
            pltpu.VMEM((4, 128, 4096), BF16),
            pltpu.VMEM((4, 2048, 128), BF16),
            pltpu.VMEM((4, 128, c), BF16),
            *reduce_scratch(64, c),
            dma((5,)), dma((30,)), dma((30,)), dma((30,)), dma((30,)), dma((4,)), dma((16,)), dma((16,)), dma((6,)),
        ],
        compiler_params=pltpu.CompilerParams(
            collective_id=0, has_side_effects=True, vmem_limit_bytes=60 * 1024 * 1024
        ),
        name="leaf_level",
    )(load_leaf, load_branch.reshape(4, 128, c), load_root.reshape(4, 64, c), inverse_leaf, coupling_leaf)
    field_branch, z_branch = pl.pallas_call(
        branch_kernel,
        out_shape=(jax.ShapeDtypeStruct((2, 256, c), F32), jax.ShapeDtypeStruct((2, 256, c), BF16)),
        in_specs=[smem] * 2 + [anywhere] * 3,
        out_specs=(vmem, vmem),
        scratch_shapes=[
            pltpu.VMEM((2, 256, 8192), BF16),
            pltpu.VMEM((32, 4, 128, c), BF16),
            pltpu.VMEM((4, 4, 4, 64, c), BF16),
            pltpu.VMEM((256, 1024), BF16),
            dma((20,)),
        ],
        compiler_params=pltpu.CompilerParams(vmem_limit_bytes=60 * 1024 * 1024),
        name="branch_level",
    )(blocks_leaf, parents, inverse_branch, b_branch, u_all)
    partial_root, u2 = pl.pallas_call(
        upper_kernel,
        out_shape=(jax.ShapeDtypeStruct((256, c), F32), jax.ShapeDtypeStruct((32, 4, 32, c), BF16)),
        in_specs=[anywhere] * 4,
        out_specs=(vmem, anywhere),
        scratch_shapes=[
            pltpu.VMEM((2, 256, c), BF16),
            pltpu.VMEM((2, 2048, 256), BF16),
            pltpu.VMEM((256, 8192), BF16),
            pltpu.VMEM((32, 4, 64, c), BF16),
            *reduce_scratch(32, c),
            dma((2,)), dma((30,)), dma((1,)), dma((16,)), dma((16,)), dma((5,)),
        ],
        compiler_params=pltpu.CompilerParams(
            collective_id=1, has_side_effects=True, vmem_limit_bytes=60 * 1024 * 1024
        ),
        name="branch_updates",
    )(z_branch, coupling_branch, inverse_root, b_root)
    field_root = pl.pallas_call(
        root_kernel,
        out_shape=jax.ShapeDtypeStruct((256, c), F32),
        in_specs=[smem] * 2 + [anywhere] * 3 + [vmem],
        out_specs=vmem,
        scratch_shapes=[
            pltpu.VMEM((256, 8192), BF16),
            pltpu.VMEM((4, 4, 4, 64, c), BF16),
            pltpu.VMEM((32, 4, 32, c), BF16),
            pltpu.VMEM((256, 1024), BF16),
            dma((6,)),
        ],
        compiler_params=pltpu.CompilerParams(vmem_limit_bytes=60 * 1024 * 1024),
        name="root_level",
    )(blocks_branch, blocks_leaf, inverse_root, u_all, u2, partial_root)
    coverage_root, coverage_branch, coverage_leaf = lax.psum(
        (
            jnp.sum(field_root * field_root, axis=-1),
            jnp.sum(field_branch * field_branch, axis=-1),
            jnp.sum(field_leaf * field_leaf, axis=-1),
        ),
        "src",
    )
    return (field_root, field_branch, field_leaf, coverage_root, coverage_branch, coverage_leaf)


def solution(mesh):
    return jax.shard_map(
        local,
        mesh=mesh,
        in_specs=(
            P("row", "src"),
            P(None, "row", "src"),
            P(None, "row", "src"),
            P("row", None),
            P(None, "row", None),
            P(None, "row", None),
            P(None, None, "row"),
            P(None, None, "row"),
            P(),
            P(),
            P(),
        ),
        out_specs=(
            P("row", "src"),
            P(None, "row", "src"),
            P(None, "row", "src"),
            P("row"),
            P(None, "row"),
            P(None, "row"),
        ),
        check_vma=False,
    )
```

time: 563 us -> 215 us (0.38)
  waiting for transfers between devices: 425 us -> 0 us
  Pallas kernels: 0 us -> 200 us
  other arithmetic: 41.3 us -> 1.41 us
  matrix products: 35.2 us -> 0 us
  local copies, waits for them, and re-layouts: 35.6 us -> 0.89 us
  between operations: 13.9 us -> 0.71 us
    psum x2 -> x0, waiting for transfers between devices: 240 us -> none  [the longest x1 131 us: local(): leaf_total = lax.psum(leaf_terms, 'row')]
    pallas_call x0 -> x4, Pallas kernels: none -> 200 us  [the longest x1 133 us: local(): pl.pallas_call(leaf_kernel, out_shape=(jax.ShapeDtypeStruct((4, 128, c),...]
    all_gather x3 -> x0, waiting for transfers between devices: 185 us -> none  [the longest x1 69.1 us: local(): lax.all_gather(branch_y, 'row', axis=1, tiled=True)]
    dot_general x5 -> x0, matrix products: 35.2 us -> none  [the longest x3 25.2 us: solve_piece(): jnp.einsum('nrw,nwc->nrc', inverse, part_rows, preferred_element_type=jnp...]
    scatter-add x2 -> x0, other arithmetic: 28.9 us -> none  [place_blocks(): buckets = buckets.at[target].add(values, mode='drop')]
    slice x3 -> x0, local copies, waits for them, and re-layouts: 25 us -> none  [the longest x2 18.5 us: local(): to_root = leaf_total[:, half_rows:]]
    concatenate x1 -> x0, other arithmetic: 10.6 us -> none  [local(): jnp.concatenate([to_root.reshape(-1, BLOCK_ROWS, source_count), branch_to...]
    dot_general x1 -> x0, local copies, waits for them, and re-layouts: 6.58 us -> none  [local(): jnp.einsum('nrw,nwc->nrc', coupling_branch, field_branch.astype(jnp.bfloa...]
  transfers between devices with their start and end apart: 5 -> 0, of which waited for: 5 -> 0; matrix products, arithmetic and copies ran while one was open for 1% -> 0% of each run, Pallas kernels for 0% -> 0%
where the time goes in v1:
time: 215 us
  Pallas kernels  200 us (93%)
  blocking collectives  11.4 us (5%)
    pallas_call x1, Pallas kernels, local(): pl.pallas_call(leaf_kernel, out_shape=(jax.ShapeDtypeStruct((4, 128, c),...  133 us
    pallas_call x1, Pallas kernels, local(): pl.pallas_call(upper_kernel, out_shape=(jax.ShapeDtypeStruct((256, c), F3...  46.5 us
    pallas_call x1, Pallas kernels, local(): pl.pallas_call(branch_kernel, out_shape=(jax.ShapeDtypeStruct((2, 256, c)...  11.6 us
    psum x1, blocking collectives, local(): lax.psum((jnp.sum(field_root * field_root, axis=-1), jnp.sum(field_branch...  11.4 us
    pallas_call x1, Pallas kernels, local(): pl.pallas_call(root_kernel, out_shape=jax.ShapeDtypeStruct((256, c), F32)...  9.48 us

profile of v1, /device:TPU:0, one launch (start us, length us, event | category | flops | bytes accessed | tf_op | source)
XLA Modules:
  0.0 214.6 jit_solution(233989746929345887)
XLA Ops:
  0.6 132.7 %leaf_level.1 = (f32[4,128,384]{2,1,0:T(8,128)}, bf16[32,4,128,384]{3,2,1,0:T(8,128)(2,1)}, bf16[32,4,64,384]{3,2,1,0:T(8,128)(2,1)}, bf16[32,4,64,384]{3,2,1,0:T(8,128)(2,1)}) custom-call(bf16[4,128,384]{2,1,0:T(8,128)(2,1)} %load_leaf.1, bf16[4,128,384]{2,1,0:T(8,128)(2,1)} %bitcast.2, bf16[4,64,384]{2,1,0:T(8,128)(2,1)} %bitcast.3, ...), custom_call_target="tpu_custom_call" | custom-call | tf_op jit(solution)/shard_map/leaf_level/pallas_call | solution.py:409
  133.3 11.6 %branch_level.1 = (f32[2,256,384]{2,1,0:T(8,128)}, bf16[2,256,384]{2,1,0:T(8,128)(2,1)}) custom-call(s32[4,16]{1,0:T(4,128)} %blocks_leaf.3, s32[4]{0:T(128)} %parents.1, bf16[2,256,8192]{2,1,0:T(8,128)(2,1)} %a_branch.1, bf16[32,4,128,384]{3,2,1,0:T(8,128)(2,1)} %get-tuple-element.15.b_branch, bf16[32,4,64,384]{3,2,1,0:T(8,128)(2,1)} %get-tuple-element.14.u_all), custom_call_target="tpu_custom_call" | custom-call | tf_op jit(solution)/shard_map/branch_level/pallas_call | solution.py:432
  144.9 46.5 %branch_updates.1 = (f32[256,384]{1,0:T(8,128)}, bf16[32,4,32,384]{3,2,1,0:T(8,128)(2,1)}) custom-call(bf16[2,256,384]{2,1,0:T(8,128)(2,1)} %get-tuple-element.16.z_in, bf16[2,2048,256]{2,1,0:T(8,128)(2,1)} %c_branch.1, bf16[256,8192]{1,0:T(8,128)(2,1)} %a_root.3, bf16[32,4,64,384]{3,2,1,0:T(8,128)(2,1)} %get-tuple-element.17.b_root), custom_call_target="tpu_custom_call" | custom-call | tf_op jit(solution)/shard_map/branch_updates/pallas_call | solution.py:447
  191.4 0.0 copy-start.1
  191.4 0.0 copy-start
  191.4 9.5 %root_level.1 = f32[256,384]{1,0:T(8,128)} custom-call(s32[2,16]{1,0:T(2,128)} %blocks_branch.1, s32[4,16]{1,0:T(4,128)} %blocks_leaf.3, bf16[256,8192]{1,0:T(8,128)(2,1)} %a_root.3, bf16[32,4,64,384]{3,2,1,0:T(8,128)(2,1)} %get-tuple-element.14.u_all, bf16[32,4,32,384]{3,2,1,0:T(8,128)(2,1)} %get-tuple-element.18.u2_in, f32[256,384]{1,0:T(8,128)} %get-tuple-element.19.partial), custom_call_target="tpu_custom_call" | custom-call | tf_op jit(solution)/shard_map/root_level/pallas_call | solution.py:465
  200.9 1.1 multiply_reduce_fusion.2
  202.0 0.0 copy-done.1
  202.0 0.1 multiply_reduce_fusion.1
  202.2 0.0 copy-done
  202.2 0.1 multiply_reduce_fusion
  202.4 11.4 %all-reduce = (f32[256]{0:T(256)}, f32[2,256]{1,0:T(2,128)}, f32[4,128]{1,0:T(4,128)}) all-reduce(f32[256]{0:T(256)S(1)} %multiply_reduce_fusion.2, f32[2,256]{1,0:T(2,128)S(1)} %multiply_reduce_fusion.1, f32[4,128]{1,0:T(4,128)S(1)} %multiply_reduce_fusion), channel_id=1, replica_groups=mesh['src'=4,'row'=32] {'src'}, use_global_device_ids=true, to_apply=%region_1.0 | all-reduce | flops 1280 | bytes 10240 | tf_op jit(solution)/shard_map/psum | solution.py:480
  213.7 0.9 copy.18
Async XLA Ops:
  191.4 10.6 %copy-start.1 = (f32[2,256,384]{2,1,0:T(8,128)S(1)}, f32[2,256,384]{2,1,0:T(8,128)}, u32[]{:S(2)}) copy-start(f32[2,256,384]{2,1,0:T(8,128)} %get-tuple-element.32) | copy-start | bytes 2359300
  191.4 10.8 %copy-start = (f32[4,128,384]{2,1,0:T(8,128)S(1)}, f32[4,128,384]{2,1,0:T(8,128)}, u32[]{:S(2)}) copy-start(f32[4,128,384]{2,1,0:T(8,128)} %get-tuple-element.33) | copy-start | bytes 2359300

commit v2 on v1

--- a/solution.py
+++ b/solution.py
@@ -210,27 +210,27 @@
 
 
 def leaf_kernel(
-    load_leaf, load_branch, load_root, inverse, coupling,
-    field, b_branch, b_root, u_all,
-    b, a, c, z, p_send, q_recv, s, t1, t2, t3, t4, u_own,
-    send, recv_l, recv_b, recv_r, recv_u, pair, recv_s, recv_q, local,
+    load_leaf, load_branch, inverse, coupling, a_branch,
+    field, field_branch, u_all,
+    b, bb, a, ab, c, z, p_send, q_recv, s, t1, t2, t3, t4, u_own,
+    send, recv_l, recv_b, recv_u, pair, recv_s, recv_q, local,
 ):
     place = Place()
     me = place.me
+    width = b.shape[3]
     copies = [
         pltpu.make_async_copy(inverse, a, local.at[0]),
         pltpu.make_async_copy(coupling, c, local.at[1]),
         pltpu.make_async_copy(load_leaf, b.at[me], local.at[2]),
-        pltpu.make_async_copy(load_branch, b_branch.at[me], local.at[3]),
-        pltpu.make_async_copy(load_root, b_root.at[me], local.at[4]),
+        pltpu.make_async_copy(load_branch, bb.at[me], local.at[3]),
+        pltpu.make_async_copy(a_branch, ab, local.at[4]),
     ]
     for copy in copies:
         copy.start()
     place.entry()
     ag_leaf = gather(place, b, load_leaf, send.at[0], recv_l, pair.at[0])
-    ag_branch = gather(place, b_branch, load_branch, send.at[1], recv_b, pair.at[1])
-    ag_root = gather(place, b_root, load_root, send.at[2], recv_r, pair.at[2])
-    ag_u = gather(place, u_all, u_own, send.at[3], recv_u, pair.at[3])
+    ag_branch = gather(place, bb, load_branch, send.at[1], recv_b, pair.at[1])
+    ag_u = gather(place, u_all, u_own, send.at[2], recv_u, pair.at[2])
     advance(ag_leaf, 27)
     advance(ag_branch, 1)
     for copy in copies[:3]:
@@ -244,30 +244,44 @@
             @pl.loop(0, place.chip // 4 + 1)
             def _(j):
                 cols = pl.ds(pl.multiple_of(j * 1024, 1024), 1024)
-                rows = b[pl.ds(j * 8, 8), n].reshape(1024, b.shape[3])
+                rows = b[pl.ds(j * 8, 8), n].reshape(1024, width)
                 field[n] += jnp.dot(a[n, :, cols], rows, preferred_element_type=F32)
 
             z[n] = field[n].astype(BF16)
             yield
-        yield from couple(place, c, z, p_send, q_recv, s, send.at[4], recv_q, 256, 8, 4)
+        yield from couple(place, c, z, p_send, q_recv, s, send.at[3], recv_q, 256, 8, 4)
+
+    def branch():
+        trips = me // 4 + 1
+        copies[3].wait()
+        copies[4].wait()
+        field_branch[...] = jnp.zeros_like(field_branch)
+        for h in range(4):
+            for n in range(2):
+
+                @pl.loop(jnp.minimum(trips, 2 * h), jnp.minimum(trips, 2 * h + 2))
+                def _(j):
+                    cols = pl.ds(pl.multiple_of(j * 1024, 1024), 1024)
+                    rows = bb[pl.ds(j * 4, 4), 2 * n : 2 * n + 2].reshape(1024, width)
+                    field_branch[n] += jnp.dot(ab[n, :, cols], rows, preferred_element_type=F32)
+
+                yield
 
     for _ in leaf():
         advance(ag_branch, 1)
-    rs = reduce(place, s, t1, t2, t3, t4, u_own, send.at[4], recv_s)
+    rs = reduce(place, s, t1, t2, t3, t4, u_own, send.at[3], recv_s)
     for _ in rs:
         advance(ag_branch, 2)
     mine = pltpu.make_async_copy(u_own, u_all.at[me], local.at[5])
     mine.start()
     advance(ag_u, 1)
     drain(ag_branch)
-    advance(ag_root, 1)
+    work = branch()
     for _ in ag_u:
-        advance(ag_root, 1)
-    drain(ag_root)
-    await_bytes(u_all.at[0:31], send.at[4])
+        advance(work, 1)
+    drain(work)
+    await_bytes(u_all.at[0:31], send.at[3])
     mine.wait()
-    for copy in copies[3:]:
-        copy.wait()
 
 
 def correct(out, index, a_cols, ids, u_rows, ag):
@@ -277,33 +291,17 @@
 
 
 def branch_kernel(
-    blocks_leaf, parents, a_branch, b_branch, u_all,
+    blocks_leaf, parents, a_branch, u_all, partial,
     field, z,
-    ab, bb, ul, ag, sems,
+    ab, ul, ag, sems,
 ):
-    width = bb.shape[3]
-    copies = []
-    for j in range(8):
-        cols = slice(1024 * j, 1024 * j + 1024)
-        copies.append(pltpu.make_async_copy(b_branch.at[4 * j : 4 * j + 4], bb.at[4 * j : 4 * j + 4], sems.at[2 * j]))
-        copies.append(pltpu.make_async_copy(a_branch.at[:, :, cols], ab.at[:, :, cols], sems.at[2 * j + 1]))
+    copies = [pltpu.make_async_copy(a_branch, ab, sems.at[4])]
     for i in range(4):
-        copies.append(pltpu.make_async_copy(u_all.at[8 * i : 8 * i + 4], ul.at[i], sems.at[16 + i]))
+        copies.append(pltpu.make_async_copy(u_all.at[8 * i : 8 * i + 4], ul.at[i], sems.at[i]))
     for copy in copies:
         copy.start()
-    trips = lax.axis_index("row") // 4 + 1
-    field[...] = jnp.zeros_like(field)
-    for j in range(8):
-        copies[2 * j].wait()
-        copies[2 * j + 1].wait()
-
-        @pl.when(j < trips)
-        def _():
-            for n in range(2):
-                rows = bb[4 * j : 4 * j + 4, 2 * n : 2 * n + 2].reshape(1024, width)
-                field[n] += jnp.dot(ab[n, :, 1024 * j : 1024 * j + 1024], rows, preferred_element_type=F32)
-
-    for copy in copies[16:]:
+    field[...] = partial[...]
+    for copy in copies:
         copy.wait()
 
     @pl.loop(0, 4)
@@ -315,22 +313,25 @@
 
 
 def upper_kernel(
-    z_in, c_branch, a_root, b_root,
+    z_in, c_branch, a_root, load_root,
     field_root, u2,
     zb, cb, ar, br, p_send, q_recv, s, t1, t2, t3, t4, u_own,
-    send, recv_u, pair, recv_s, recv_q, local,
+    send, recv_r, recv_u, pair, recv_s, recv_q, local,
 ):
     place = Place()
     me = place.me
     width = br.shape[3]
-    pairs = ((z_in, zb), (c_branch, cb), (b_root, br), (a_root, ar))
+    pairs = ((z_in, zb), (c_branch, cb), (load_root, br.at[me]), (a_root, ar))
     copies = [pltpu.make_async_copy(src, dst, local.at[k]) for k, (src, dst) in enumerate(pairs)]
     for copy in copies:
         copy.start()
     place.entry()
+    ag_root = gather(place, br, load_root, send.at[2], recv_r, pair.at[1])
+    advance(ag_root, 1)
     copies[0].wait()
     copies[1].wait()
-    drain(couple(place, cb, zb, p_send, q_recv, s, send.at[0], recv_q, 128, 16, 1))
+    for _ in couple(place, cb, zb, p_send, q_recv, s, send.at[0], recv_q, 128, 16, 4):
+        advance(ag_root, 1)
 
     def root():
         trips = me // 4 + 1
@@ -347,14 +348,18 @@
 
             yield
 
-    work = root()
     rs = reduce(place, s, t1, t2, t3, t4, u_own, send.at[0], recv_s)
     for _ in rs:
+        advance(ag_root, 2)
+    mine = pltpu.make_async_copy(u_own, u2.at[me], local.at[4])
+    mine.start()
+    ag_u = gather(place, u2, u_own, send.at[1], recv_u, pair.at[0])
+    advance(ag_u, 1)
+    drain(ag_root)
+    work = root()
+    for _ in ag_u:
         advance(work, 1)
     drain(work)
-    mine = pltpu.make_async_copy(u_own, u2.at[me], local.at[4])
-    mine.start()
-    drain(gather(place, u2, u_own, send.at[1], recv_u, pair.at[0]))
     await_bytes(u2.at[0:31], send.at[0])
     mine.wait()
 
@@ -406,44 +411,44 @@
     anywhere = pl.BlockSpec(memory_space=pl.ANY)
     vmem = pl.BlockSpec(memory_space=pltpu.VMEM)
     smem = pl.BlockSpec(memory_space=pltpu.SMEM)
-    field_leaf, b_branch, b_root, u_all = pl.pallas_call(
+    field_leaf, partial_branch, u_all = pl.pallas_call(
         leaf_kernel,
         out_shape=(
             jax.ShapeDtypeStruct((4, 128, c), F32),
-            jax.ShapeDtypeStruct((32, 4, 128, c), BF16),
-            jax.ShapeDtypeStruct((32, 4, 64, c), BF16),
+            jax.ShapeDtypeStruct((2, 256, c), F32),
             jax.ShapeDtypeStruct((32, 4, 64, c), BF16),
         ),
         in_specs=[anywhere] * 5,
-        out_specs=(vmem, anywhere, anywhere, anywhere),
+        out_specs=(vmem, vmem, anywhere),
         scratch_shapes=[
             pltpu.VMEM((32, 4, 128, c), BF16),
+            pltpu.VMEM((32, 4, 128, c), BF16),
             pltpu.VMEM((4, 128, 4096), BF16),
+            pltpu.VMEM((2, 256, 8192), BF16),
             pltpu.VMEM((4, 2048, 128), BF16),
             pltpu.VMEM((4, 128, c), BF16),
             *reduce_scratch(64, c),
-            dma((5,)), dma((30,)), dma((30,)), dma((30,)), dma((30,)), dma((4,)), dma((16,)), dma((16,)), dma((6,)),
+            dma((4,)), dma((30,)), dma((30,)), dma((30,)), dma((3,)), dma((16,)), dma((16,)), dma((6,)),
         ],
         compiler_params=pltpu.CompilerParams(
-            collective_id=0, has_side_effects=True, vmem_limit_bytes=60 * 1024 * 1024
+            collective_id=0, has_side_effects=True, vmem_limit_bytes=62 * 1024 * 1024
         ),
         name="leaf_level",
-    )(load_leaf, load_branch.reshape(4, 128, c), load_root.reshape(4, 64, c), inverse_leaf, coupling_leaf)
+    )(load_leaf, load_branch.reshape(4, 128, c), inverse_leaf, coupling_leaf, inverse_branch)
     field_branch, z_branch = pl.pallas_call(
         branch_kernel,
         out_shape=(jax.ShapeDtypeStruct((2, 256, c), F32), jax.ShapeDtypeStruct((2, 256, c), BF16)),
-        in_specs=[smem] * 2 + [anywhere] * 3,
+        in_specs=[smem] * 2 + [anywhere] * 2 + [vmem],
         out_specs=(vmem, vmem),
         scratch_shapes=[
             pltpu.VMEM((2, 256, 8192), BF16),
-            pltpu.VMEM((32, 4, 128, c), BF16),
             pltpu.VMEM((4, 4, 4, 64, c), BF16),
             pltpu.VMEM((256, 1024), BF16),
-            dma((20,)),
+            dma((5,)),
         ],
         compiler_params=pltpu.CompilerParams(vmem_limit_bytes=60 * 1024 * 1024),
         name="branch_level",
-    )(blocks_leaf, parents, inverse_branch, b_branch, u_all)
+    )(blocks_leaf, parents, inverse_branch, u_all, partial_branch)
     partial_root, u2 = pl.pallas_call(
         upper_kernel,
         out_shape=(jax.ShapeDtypeStruct((256, c), F32), jax.ShapeDtypeStruct((32, 4, 32, c), BF16)),
@@ -455,13 +460,13 @@
             pltpu.VMEM((256, 8192), BF16),
             pltpu.VMEM((32, 4, 64, c), BF16),
             *reduce_scratch(32, c),
-            dma((2,)), dma((30,)), dma((1,)), dma((16,)), dma((16,)), dma((5,)),
+            dma((3,)), dma((30,)), dma((30,)), dma((2,)), dma((16,)), dma((16,)), dma((5,)),
         ],
         compiler_params=pltpu.CompilerParams(
             collective_id=1, has_side_effects=True, vmem_limit_bytes=60 * 1024 * 1024
         ),
         name="branch_updates",
-    )(z_branch, coupling_branch, inverse_root, b_root)
+    )(z_branch, coupling_branch, inverse_root, load_root.reshape(4, 64, c))
     field_root = pl.pallas_call(
         root_kernel,
         out_shape=jax.ShapeDtypeStruct((256, c), F32),

time: 215 us -> 204 us (0.949)
  Pallas kernels: 200 us -> 189 us
    pallas_call x1, Pallas kernels: 133 us -> 118 us  [local(): pl.pallas_call(leaf_kernel, out_shape=(jax.ShapeDtypeStruct((4, 128, c),...]
    pallas_call x1, Pallas kernels: 46.5 us -> 53.2 us  [local(): pl.pallas_call(upper_kernel, out_shape=(jax.ShapeDtypeStruct((256, c), F3...]
    pallas_call x1, Pallas kernels: 11.6 us -> 8.18 us  [local(): pl.pallas_call(branch_kernel, out_shape=(jax.ShapeDtypeStruct((2, 256, c)...]
where the time goes in v2:
time: 204 us
  Pallas kernels  189 us (93%)
  blocking collectives  11.4 us (6%)
    pallas_call x1, Pallas kernels, local(): pl.pallas_call(leaf_kernel, out_shape=(jax.ShapeDtypeStruct((4, 128, c),...  118 us
    pallas_call x1, Pallas kernels, local(): pl.pallas_call(upper_kernel, out_shape=(jax.ShapeDtypeStruct((256, c), F3...  53.2 us
    psum x1, blocking collectives, local(): lax.psum((jnp.sum(field_root * field_root, axis=-1), jnp.sum(field_branch...  11.4 us
    pallas_call x1, Pallas kernels, local(): pl.pallas_call(root_kernel, out_shape=jax.ShapeDtypeStruct((256, c), F32)...  9.5 us
    pallas_call x1, Pallas kernels, local(): pl.pallas_call(branch_kernel, out_shape=(jax.ShapeDtypeStruct((2, 256, c)...  8.18 us

profile of v2, /device:TPU:0, one launch (start us, length us, event | category | flops | bytes accessed | tf_op | source)
XLA Modules:
  0.0 203.5 jit_solution(10016335471342468562)
XLA Ops:
  0.6 118.2 %leaf_level.1 = (f32[4,128,384]{2,1,0:T(8,128)}, f32[2,256,384]{2,1,0:T(8,128)}, bf16[32,4,64,384]{3,2,1,0:T(8,128)(2,1)}) custom-call(bf16[4,128,384]{2,1,0:T(8,128)(2,1)} %load_leaf.1, bf16[4,128,384]{2,1,0:T(8,128)(2,1)} %bitcast.2, bf16[4,128,4096]{2,1,0:T(8,128)(2,1)} %inverse.1, bf16[4,2048,128]{2,1,0:T(8,128)(2,1)} %coupling.1, ...), custom_call_target="tpu_custom_call" | custom-call | tf_op jit(solution)/shard_map/leaf_level/pallas_call | solution.py:414
  118.9 8.2 %branch_level.1 = (f32[2,256,384]{2,1,0:T(8,128)}, bf16[2,256,384]{2,1,0:T(8,128)(2,1)}) custom-call(s32[4,16]{1,0:T(4,128)} %blocks_leaf.3, s32[4]{0:T(128)} %parents.1, bf16[2,256,8192]{2,1,0:T(8,128)(2,1)} %a_branch.3, bf16[32,4,64,384]{3,2,1,0:T(8,128)(2,1)} %get-tuple-element.13.u_all, f32[2,256,384]{2,1,0:T(8,128)} %get-tuple-element.14.partial), custom_call_target="tpu_custom_call" | custom-call | tf_op jit(solution)/shard_map/branch_level/pallas_call | solution.py:438
  127.1 53.2 %branch_updates.1 = (f32[256,384]{1,0:T(8,128)}, bf16[32,4,32,384]{3,2,1,0:T(8,128)(2,1)}) custom-call(bf16[2,256,384]{2,1,0:T(8,128)(2,1)} %get-tuple-element.15.z_in, bf16[2,2048,256]{2,1,0:T(8,128)(2,1)} %c_branch.1, bf16[256,8192]{1,0:T(8,128)(2,1)} %a_root.3, bf16[4,64,384]{2,1,0:T(8,128)(2,1)} %bitcast.3), custom_call_target="tpu_custom_call" | custom-call | tf_op jit(solution)/shard_map/branch_updates/pallas_call | solution.py:452
  180.3 0.0 copy-start.1
  180.3 0.0 copy-start
  180.3 9.5 %root_level.1 = f32[256,384]{1,0:T(8,128)} custom-call(s32[2,16]{1,0:T(2,128)} %blocks_branch.1, s32[4,16]{1,0:T(4,128)} %blocks_leaf.3, bf16[256,8192]{1,0:T(8,128)(2,1)} %a_root.3, bf16[32,4,64,384]{3,2,1,0:T(8,128)(2,1)} %get-tuple-element.13.u_all, bf16[32,4,32,384]{3,2,1,0:T(8,128)(2,1)} %get-tuple-element.16.u2_in, f32[256,384]{1,0:T(8,128)} %get-tuple-element.17.partial), custom_call_target="tpu_custom_call" | custom-call | tf_op jit(solution)/shard_map/root_level/pallas_call | solution.py:470
  189.8 1.1 multiply_reduce_fusion.2
  190.9 0.0 copy-done.1
  190.9 0.1 multiply_reduce_fusion.1
  191.1 0.0 copy-done
  191.1 0.1 multiply_reduce_fusion
  191.3 11.4 %all-reduce = (f32[256]{0:T(256)}, f32[2,256]{1,0:T(2,128)}, f32[4,128]{1,0:T(4,128)}) all-reduce(f32[256]{0:T(256)S(1)} %multiply_reduce_fusion.2, f32[2,256]{1,0:T(2,128)S(1)} %multiply_reduce_fusion.1, f32[4,128]{1,0:T(4,128)S(1)} %multiply_reduce_fusion), channel_id=1, replica_groups=mesh['src'=4,'row'=32] {'src'}, use_global_device_ids=true, to_apply=%region_1.0 | all-reduce | flops 1280 | bytes 10240 | tf_op jit(solution)/shard_map/psum | solution.py:485
  202.7 0.9 copy.18
Async XLA Ops:
  180.3 10.6 %copy-start.1 = (f32[2,256,384]{2,1,0:T(8,128)S(1)}, f32[2,256,384]{2,1,0:T(8,128)}, u32[]{:S(2)}) copy-start(f32[2,256,384]{2,1,0:T(8,128)} %get-tuple-element.30) | copy-start | bytes 2359300
  180.3 10.8 %copy-start = (f32[4,128,384]{2,1,0:T(8,128)S(1)}, f32[4,128,384]{2,1,0:T(8,128)}, u32[]{:S(2)}) copy-start(f32[4,128,384]{2,1,0:T(8,128)} %get-tuple-element.31) | copy-start | bytes 2359300

commit v3 on v2

--- a/solution.py
+++ b/solution.py
@@ -291,17 +291,22 @@
 
 
 def branch_kernel(
-    blocks_leaf, parents, a_branch, u_all, partial,
-    field, z,
-    ab, ul, ag, sems,
+    blocks_leaf, blocks_branch, parents, a_branch, a_root, u_all, partial,
+    field, z, root_cols,
+    ab, ar, ul, ag, sems,
 ):
-    copies = [pltpu.make_async_copy(a_branch, ab, sems.at[4])]
+    copies = [pltpu.make_async_copy(a_root, ar, sems.at[5]), pltpu.make_async_copy(a_branch, ab, sems.at[4])]
     for i in range(4):
         copies.append(pltpu.make_async_copy(u_all.at[8 * i : 8 * i + 4], ul.at[i], sems.at[i]))
     for copy in copies:
         copy.start()
     field[...] = partial[...]
-    for copy in copies:
+    copies[0].wait()
+    blocks = [blocks_leaf[i, 8 + k] - 64 for i in range(4) for k in range(8)]
+    blocks += [blocks_branch[p, k] for p in range(2) for k in range(16)]
+    for slot, block in enumerate(blocks):
+        root_cols[:, slot * 128 : slot * 128 + 128] = ar[:, pl.ds(pl.multiple_of(block * 128, 128), 128)]
+    for copy in copies[1:]:
         copy.wait()
 
     @pl.loop(0, 4)
@@ -313,16 +318,18 @@
 
 
 def upper_kernel(
-    z_in, c_branch, a_root, load_root,
-    field_root, u2,
-    zb, cb, ar, br, p_send, q_recv, s, t1, t2, t3, t4, u_own,
+    z_in, c_branch, a_root, load_root, root_cols, u_all,
+    field_root,
+    zb, cb, ar, br, cols_root, ul, u2, p_send, q_recv, s, t1, t2, t3, t4, u_own,
     send, recv_r, recv_u, pair, recv_s, recv_q, local,
 ):
     place = Place()
     me = place.me
     width = br.shape[3]
-    pairs = ((z_in, zb), (c_branch, cb), (load_root, br.at[me]), (a_root, ar))
+    pairs = ((z_in, zb), (c_branch, cb), (load_root, br.at[me]), (a_root, ar), (root_cols, cols_root))
     copies = [pltpu.make_async_copy(src, dst, local.at[k]) for k, (src, dst) in enumerate(pairs)]
+    for i in range(4):
+        copies.append(pltpu.make_async_copy(u_all.at[8 * i + 4 : 8 * i + 8], ul.at[i], local.at[6 + i]))
     for copy in copies:
         copy.start()
     place.entry()
@@ -347,11 +354,20 @@
                 field_root[...] += jnp.dot(ar[:, cols], rows, preferred_element_type=F32)
 
             yield
+        for copy in copies[4:]:
+            copy.wait()
+        for i in range(4):
+            correct(i, ul[i])
+            yield
+
+    def correct(chunk, u_rows):
+        cols = cols_root[:, chunk * 1024 : chunk * 1024 + 1024]
+        field_root[...] -= jnp.dot(cols, u_rows.reshape(1024, width), preferred_element_type=F32)
 
     rs = reduce(place, s, t1, t2, t3, t4, u_own, send.at[0], recv_s)
     for _ in rs:
         advance(ag_root, 2)
-    mine = pltpu.make_async_copy(u_own, u2.at[me], local.at[4])
+    mine = pltpu.make_async_copy(u_own, u2.at[me], local.at[5])
     mine.start()
     ag_u = gather(place, u2, u_own, send.at[1], recv_u, pair.at[0])
     advance(ag_u, 1)
@@ -360,33 +376,10 @@
     for _ in ag_u:
         advance(work, 1)
     drain(work)
+    mine.wait()
+    for q in range(4):
+        correct(4 + q, u2[8 * q : 8 * q + 8])
     await_bytes(u2.at[0:31], send.at[0])
-    mine.wait()
-
-
-def root_kernel(
-    blocks_branch, blocks_leaf, a_root, u_all, u2_in, partial,
-    field,
-    ar, ul, ub, ag, sems,
-):
-    copies = [pltpu.make_async_copy(a_root, ar, sems.at[0]), pltpu.make_async_copy(u2_in, ub, sems.at[1])]
-    for i in range(4):
-        copies.append(pltpu.make_async_copy(u_all.at[8 * i + 4 : 8 * i + 8], ul.at[i], sems.at[2 + i]))
-    for copy in copies:
-        copy.start()
-    field[...] = partial[...]
-    for copy in copies:
-        copy.wait()
-
-    @pl.loop(0, 4)
-    def _(i):
-        correct(field, ..., lambda col: ar[:, pl.ds(col, 128)], lambda k: blocks_leaf[i, 8 + k] - 64, ul[i], ag)
-
-    @pl.loop(0, 4)
-    def _(i):
-        p, h = i // 2, lax.rem(i, 2)
-        rows = ub[pl.ds(i * 8, 8)]
-        correct(field, ..., lambda col: ar[:, pl.ds(col, 128)], lambda k: blocks_branch[p, 8 * h + k], rows, ag)
 
 
 def reduce_scratch(q, c):
@@ -435,53 +428,46 @@
         ),
         name="leaf_level",
     )(load_leaf, load_branch.reshape(4, 128, c), inverse_leaf, coupling_leaf, inverse_branch)
-    field_branch, z_branch = pl.pallas_call(
+    field_branch, z_branch, root_cols = pl.pallas_call(
         branch_kernel,
-        out_shape=(jax.ShapeDtypeStruct((2, 256, c), F32), jax.ShapeDtypeStruct((2, 256, c), BF16)),
-        in_specs=[smem] * 2 + [anywhere] * 2 + [vmem],
-        out_specs=(vmem, vmem),
+        out_shape=(
+            jax.ShapeDtypeStruct((2, 256, c), F32),
+            jax.ShapeDtypeStruct((2, 256, c), BF16),
+            jax.ShapeDtypeStruct((256, 8192), BF16),
+        ),
+        in_specs=[smem] * 3 + [anywhere] * 3 + [vmem],
+        out_specs=(vmem, vmem, vmem),
         scratch_shapes=[
             pltpu.VMEM((2, 256, 8192), BF16),
+            pltpu.VMEM((256, 8192), BF16),
             pltpu.VMEM((4, 4, 4, 64, c), BF16),
             pltpu.VMEM((256, 1024), BF16),
-            dma((5,)),
+            dma((6,)),
         ],
         compiler_params=pltpu.CompilerParams(vmem_limit_bytes=60 * 1024 * 1024),
         name="branch_level",
-    )(blocks_leaf, parents, inverse_branch, u_all, partial_branch)
-    partial_root, u2 = pl.pallas_call(
+    )(blocks_leaf, blocks_branch, parents, inverse_branch, inverse_root, u_all, partial_branch)
+    field_root = pl.pallas_call(
         upper_kernel,
-        out_shape=(jax.ShapeDtypeStruct((256, c), F32), jax.ShapeDtypeStruct((32, 4, 32, c), BF16)),
-        in_specs=[anywhere] * 4,
-        out_specs=(vmem, anywhere),
+        out_shape=jax.ShapeDtypeStruct((256, c), F32),
+        in_specs=[anywhere] * 6,
+        out_specs=vmem,
         scratch_shapes=[
             pltpu.VMEM((2, 256, c), BF16),
             pltpu.VMEM((2, 2048, 256), BF16),
             pltpu.VMEM((256, 8192), BF16),
             pltpu.VMEM((32, 4, 64, c), BF16),
+            pltpu.VMEM((256, 8192), BF16),
+            pltpu.VMEM((4, 4, 4, 64, c), BF16),
+            pltpu.VMEM((32, 4, 32, c), BF16),
             *reduce_scratch(32, c),
-            dma((3,)), dma((30,)), dma((30,)), dma((2,)), dma((16,)), dma((16,)), dma((5,)),
+            dma((3,)), dma((30,)), dma((30,)), dma((2,)), dma((16,)), dma((16,)), dma((10,)),
         ],
         compiler_params=pltpu.CompilerParams(
             collective_id=1, has_side_effects=True, vmem_limit_bytes=60 * 1024 * 1024
         ),
-        name="branch_updates",
-    )(z_branch, coupling_branch, inverse_root, load_root.reshape(4, 64, c))
-    field_root = pl.pallas_call(
-        root_kernel,
-        out_shape=jax.ShapeDtypeStruct((256, c), F32),
-        in_specs=[smem] * 2 + [anywhere] * 3 + [vmem],
-        out_specs=vmem,
-        scratch_shapes=[
-            pltpu.VMEM((256, 8192), BF16),
-            pltpu.VMEM((4, 4, 4, 64, c), BF16),
-            pltpu.VMEM((32, 4, 32, c), BF16),
-            pltpu.VMEM((256, 1024), BF16),
-            dma((6,)),
-        ],
-        compiler_params=pltpu.CompilerParams(vmem_limit_bytes=60 * 1024 * 1024),
         name="root_level",
-    )(blocks_branch, blocks_leaf, inverse_root, u_all, u2, partial_root)
+    )(z_branch, coupling_branch, inverse_root, load_root.reshape(4, 64, c), root_cols, u_all)
     coverage_root, coverage_branch, coverage_leaf = lax.psum(
         (
             jnp.sum(field_root * field_root, axis=-1),

time: 204 us -> 199 us (0.975)
  Pallas kernels: 189 us -> 183 us
    pallas_call x2 -> x1, Pallas kernels: 62.7 us -> 53.4 us  [local(): pl.pallas_call(upper_kernel, out_shape=jax.ShapeDtypeStruct((256, c), F32...]
    pallas_call x1, Pallas kernels: 8.18 us -> 10.9 us  [local(): pl.pallas_call(branch_kernel, out_shape=(jax.ShapeDtypeStruct((2, 256, c)...]
where the time goes in v3:
time: 199 us
  Pallas kernels  183 us (92%)
  blocking collectives  11.4 us (6%)
  local copies, waits for them, and re-layouts  2.66 us (1%)
    pallas_call x1, Pallas kernels, local(): pl.pallas_call(leaf_kernel, out_shape=(jax.ShapeDtypeStruct((4, 128, c),...  118 us
    pallas_call x1, Pallas kernels, local(): pl.pallas_call(upper_kernel, out_shape=jax.ShapeDtypeStruct((256, c), F32...  53.4 us
    psum x1, blocking collectives, local(): lax.psum((jnp.sum(field_root * field_root, axis=-1), jnp.sum(field_branch...  11.4 us
    pallas_call x1, Pallas kernels, local(): pl.pallas_call(branch_kernel, out_shape=(jax.ShapeDtypeStruct((2, 256, c)...  10.9 us

profile of v3, /device:TPU:0, one launch (start us, length us, event | category | flops | bytes accessed | tf_op | source)
XLA Modules:
  0.0 198.7 jit_solution(2858816419666604504)
XLA Ops:
  0.6 118.3 %leaf_level.1 = (f32[4,128,384]{2,1,0:T(8,128)}, f32[2,256,384]{2,1,0:T(8,128)}, bf16[32,4,64,384]{3,2,1,0:T(8,128)(2,1)}) custom-call(bf16[4,128,384]{2,1,0:T(8,128)(2,1)} %load_leaf.1, bf16[4,128,384]{2,1,0:T(8,128)(2,1)} %bitcast.2, bf16[4,128,4096]{2,1,0:T(8,128)(2,1)} %inverse.1, bf16[4,2048,128]{2,1,0:T(8,128)(2,1)} %coupling.1, ...), custom_call_target="tpu_custom_call" | custom-call | tf_op jit(solution)/shard_map/leaf_level/pallas_call | solution.py:407
  118.9 10.9 %branch_level.1 = (f32[2,256,384]{2,1,0:T(8,128)}, bf16[2,256,384]{2,1,0:T(8,128)(2,1)}, bf16[256,8192]{1,0:T(8,128)(2,1)}) custom-call(s32[4,16]{1,0:T(4,128)} %blocks_leaf.1, s32[2,16]{1,0:T(2,128)} %blocks_branch.1, s32[4]{0:T(128)} %parents.1, bf16[2,256,8192]{2,1,0:T(8,128)(2,1)} %a_branch.3, bf16[256,8192]{1,0:T(8,128)(2,1)} %a_root.3, ...), custom_call_target="tpu_custom_call" | custom-call | tf_op jit(solution)/shard_map/branch_level/pallas_call | solution.py:431
  129.8 0.0 copy-start.1
  129.8 0.0 copy-start
  129.8 53.4 %root_level.1 = f32[256,384]{1,0:T(8,128)} custom-call(bf16[2,256,384]{2,1,0:T(8,128)(2,1)} %get-tuple-element.14.z_in, bf16[2,2048,256]{2,1,0:T(8,128)(2,1)} %c_branch.1, bf16[256,8192]{1,0:T(8,128)(2,1)} %a_root.3, bf16[4,64,384]{2,1,0:T(8,128)(2,1)} %bitcast.3, bf16[256,8192]{1,0:T(8,128)(2,1)} %get-tuple-element.15.root_cols, ...), custom_call_target="tpu_custom_call" | custom-call | tf_op jit(solution)/shard_map/root_level/pallas_call | solution.py:450
  183.2 1.1 multiply_reduce_fusion.2
  184.3 0.0 copy-done.1
  184.4 0.1 multiply_reduce_fusion.1
  184.5 0.0 copy-done
  184.5 0.1 multiply_reduce_fusion
  184.7 11.4 %all-reduce = (f32[256]{0:T(256)}, f32[2,256]{1,0:T(2,128)}, f32[4,128]{1,0:T(4,128)}) all-reduce(f32[256]{0:T(256)S(1)} %multiply_reduce_fusion.2, f32[2,256]{1,0:T(2,128)S(1)} %multiply_reduce_fusion.1, f32[4,128]{1,0:T(4,128)S(1)} %multiply_reduce_fusion), channel_id=1, replica_groups=mesh['src'=4,'row'=32] {'src'}, use_global_device_ids=true, to_apply=%region_1.0 | all-reduce | flops 1280 | bytes 10240 | tf_op jit(solution)/shard_map/psum | solution.py:471
  196.1 1.8 copy.19
  197.8 0.9 copy.20
Async XLA Ops:
  129.8 54.5 %copy-start.1 = (f32[2,256,384]{2,1,0:T(8,128)S(1)}, f32[2,256,384]{2,1,0:T(8,128)}, u32[]{:S(2)}) copy-start(f32[2,256,384]{2,1,0:T(8,128)} %get-tuple-element.28) | copy-start | bytes 2359300
  129.8 54.7 %copy-start = (f32[4,128,384]{2,1,0:T(8,128)S(1)}, f32[4,128,384]{2,1,0:T(8,128)}, u32[]{:S(2)}) copy-start(f32[4,128,384]{2,1,0:T(8,128)} %get-tuple-element.29) | copy-start | bytes 2359300
